TPU v7x, 256 devices: a whole 4x4x8 slice. The times are simulated.
256 devices in a mesh: dom: 64 (over z, x, core), feat: 4 (over y).
Axes of the slice: x: 4, y: 4, z: 8, core: 2. Of those that a mesh axis runs over, the one named last changes fastest.
Arguments:
- features: float32 [98304, 1024], P('dom', 'feat'), may hold values from -6 to 6
- degree: int32 [98304], P('dom'), may hold values from 1 to 9
- diag_adj: float32 [98304, 128], P('dom'), may hold values from -0.25 to 0.25
- remote_adj: float32 [64, 48, 128, 128], P('dom'), may hold values from -0.25 to 0.25
- read_block: int32 [64, 64], P('dom'), may hold values from 0 to 12, as said below
- tile_src: int32 [64, 48], P('dom'), may hold values from 0 to 63, as said below
- tile_row: int32 [64, 48], P('dom'), may hold values from 0 to 11, as said below
- w_first: float32 [1024, 1024], P('feat'), may hold values from -0.25 to 0.25
- b_first: float32 [1024], replicated, may hold values from -2 to 2
- w_second: float32 [1024, 1024], P('feat'), may hold values from -0.25 to 0.25
- b_second: float32 [1024], replicated, may hold values from -2 to 2
Outputs:
- embed: float32 [98304, 1024], P(('dom', 'feat'))
Inputs may be any that keep to these rules, and one draw needn't show every extreme that they name: `read_block`: entry [s, d] is the block of partition s that partition d reads, or 12 if d does not read s. Every partition reads exactly 24 other partitions, one block of each, and never itself. `tile_src`: tiles come in groups of 2 consecutive tiles with the same source partition; the sources of a partition's tiles are exactly the 24 partitions that it reads according to read_block. `tile_row`: within a group of 2 tiles with the same source, the block rows are distinct.
All inputs are finite; a program needn't handle non-finite values.
Results may differ from a plain program's by a relative error of at most 0.0003.
Values sent between devices are 32-bit elements; how exact they have to be, the bound alone decides.
A program may use at most 128 MiB of HBM per device.

v0:
```python
import jax
import jax.numpy as jnp
from jax import lax
from jax.sharding import PartitionSpec as P


def aggregate(features_slice, scaling, diag_adj, remote_adj, read_block, tile_src, tile_row):
    tile_size = diag_adj.shape[1]
    block_count = diag_adj.shape[0] // tile_size
    columns = features_slice.shape[1]
    levels = jnp.arange(block_count, dtype=jnp.int32)
    scaled = features_slice * scaling[:, None]
    block_rows = scaled.reshape(block_count, tile_size, columns)
    choose = (read_block[0][:, None] == levels[None, :]).astype(jnp.float32)
    outgoing = jnp.einsum("db,btf->dtf", choose, block_rows, precision=lax.Precision.HIGHEST)
    incoming = lax.all_to_all(outgoing, "dom", split_axis=0, concat_axis=0, tiled=True)
    picked = incoming[tile_src[0]]
    products = jnp.einsum("kij,kjf->kif", remote_adj[0], picked, precision=lax.Precision.HIGHEST)
    row_onehot = (tile_row[0][None, :] == levels[:, None]).astype(jnp.float32)
    remote_sum = jnp.einsum("bk,kif->bif", row_onehot, products, precision=lax.Precision.HIGHEST)
    own = jnp.einsum(
        "bij,bjf->bif",
        diag_adj.reshape(block_count, tile_size, tile_size),
        block_rows,
        precision=lax.Precision.HIGHEST,
    )
    return (own + remote_sum).reshape(-1, columns) * scaling[:, None]


def transform(aggregated, weight_rows, bias, rectify):
    vertices = lax.all_to_all(aggregated, "feat", split_axis=0, concat_axis=1, tiled=True)
    mixed = jnp.dot(
        vertices,
        lax.all_gather(weight_rows, "feat", axis=0, tiled=True),
        precision=lax.Precision.HIGHEST,
        preferred_element_type=jnp.float32,
    )
    mixed = mixed + bias[None, :]
    if rectify:
        mixed = jnp.maximum(mixed, 0.0)
    return mixed


def per_device(
    features,
    degree,
    diag_adj,
    remote_adj,
    read_block,
    tile_src,
    tile_row,
    w_first,
    b_first,
    w_second,
    b_second,
):
    scaling = lax.rsqrt(degree.astype(jnp.float32))
    first_sum = aggregate(features, scaling, diag_adj, remote_adj, read_block, tile_src, tile_row)
    hidden = transform(first_sum, w_first, b_first, True)
    hidden_slice = lax.all_to_all(hidden, "feat", split_axis=1, concat_axis=0, tiled=True)
    second_sum = aggregate(
        hidden_slice, scaling, diag_adj, remote_adj, read_block, tile_src, tile_row
    )
    return transform(second_sum, w_second, b_second, False)


def solution(mesh):
    return jax.shard_map(
        per_device,
        mesh=mesh,
        in_specs=(
            P("dom", "feat"),
            P("dom"),
            P("dom", None),
            P("dom", None, None, None),
            P("dom", None),
            P("dom", None),
            P("dom", None),
            P("feat", None),
            P(),
            P("feat", None),
            P(),
        ),
        out_specs=P(("dom", "feat"), None),
        check_vma=False,
    )
```

profile of v0, /device:TPU:33, one launch (start us, length us, event | category | flops | bytes accessed | tf_op | source)
XLA Modules:
  0.0 610.4 jit_solution(18088798726562840623)
XLA Ops:
  6.5 0.0 copy-start
  6.5 0.0 copy-start.9
  6.5 0.9 fusion.30
  7.4 1.8 broadcast_multiply_fusion.2
  9.2 0.0 copy-start.1
  9.2 1.1 copy-done.1
  10.3 0.0 copy-done.9
  10.3 3.7 fusion.10
  14.1 8.1 %copy.48 = f32[64,128,256]{2,1,0:T(8,128)} copy(f32[64,128,256]{2,0,1:T(8,128)S(1)} %fusion.10) | data formatting | bytes 16777216 | tf_op jit(solution)/shard_map/db,btf->dtf/dot_general | solution.py:15
  22.1 0.0 copy-start.10
  22.1 12.2 %all-to-all-start = ((f32[64,128,256]{2,1,0:T(8,128)}), f32[64,128,256]{2,1,0:T(8,128)}, u32[]{:S(2)}, u32[]{:S(2)}) async-start(f32[64,128,256]{2,1,0:T(8,128)} %copy.48), calls=%async_computation | async-start | bytes 16777216 | tf_op jit(solution)/shard_map/all_to_all | solution.py:16
  34.3 0.2 all-gather.3.cloned.1.call-start
  34.6 0.5 all-gather.3.cloned.1.call-update
  35.1 0.0 copy-done.10
  35.1 184.9 %all-to-all-done = f32[64,128,256]{2,1,0:T(8,128)} async-done(((f32[64,128,256]{2,1,0:T(8,128)}), f32[64,128,256]{2,1,0:T(8,128)}, u32[]{:S(2)}, u32[]{:S(2)}) %all-to-all-start) | async-done | bytes 8388640 | tf_op jit(solution)/shard_map/all_to_all | solution.py:16
  220.1 7.0 %gather_fusion = f32[48,128,256]{2,1,0:T(8,128)} fusion(f32[64,128,256]{2,1,0:T(8,128)} %all-to-all-done, s32[1024]{0:T(1024)S(1)} %pad_clamp_fusion), kind=kCustom, calls=%fused_computation | custom fusion | bytes 12583104 | tf_op jit(solution)/shard_map/gather | solution.py:17
  227.1 0.0 copy-done
  227.1 14.3 %fusion.4 = f32[48,128,256]{1,2,0:T(8,128)} fusion(f32[48,128,256]{2,1,0:T(8,128)} %gather_fusion, f32[1,48,128,128]{3,2,1,0:T(8,128)S(1)} %copy-done), kind=kOutput, calls=%fused_computation.6 | convolution fusion | flops 2415919104 | bytes 15728640 | tf_op jit(solution)/shard_map/kij,kjf->kif/dot_general | solution.py:18
  241.3 0.0 copy-start.8
  241.3 6.7 %copy.50 = f32[48,128,256]{2,0,1:T(8,128)} copy(f32[48,128,256]{1,2,0:T(8,128)} %fusion.4) | data formatting | bytes 12582912 | tf_op jit(solution)/shard_map/kij,kjf->kif/dot_general | solution.py:18
  248.0 0.0 copy-done.8
  248.0 0.0 copy-start.2
  248.0 0.0 copy-start.4
  248.1 4.4 fusion.19
  252.5 0.0 copy-done.2
  252.5 0.0 copy-done.4
  252.5 3.5 bitcast_add_fusion.1
  256.0 3.1 copy.52
  259.1 2.7 broadcast_multiply_fusion.1
  261.7 0.0 copy-start.6
  261.7 4.5 all-to-all-start.1
  266.2 0.0 all-gather.3.cloned.1.call-done
  266.3 19.8 %all-to-all-done.1 = f32[4,384,256]{1,2,0:T(8,128)} async-done(((f32[4,384,256]{1,2,0:T(8,128)}), f32[4,384,256]{1,2,0:T(8,128)}, u32[]{:S(2)}, u32[]{:S(2)}) %all-to-all-start.1) | async-done | bytes 1572896 | tf_op jit(solution)/shard_map/all_to_all | solution.py:31
  286.1 0.0 copy-done.6
  286.1 7.6 %add_maximum_fusion = f32[384,1024]{1,0:T(8,128)S(1)} fusion(f32[384,1024]{0,1:T(8,128)} %bitcast.13, f32[1024,1024]{1,0:T(8,128)} %all-gather.3.cloned.1.call-done, f32[1024]{0:T(1024)S(1)} %copy-done.6), kind=kOutput, calls=%fused_computation.16 | convolution fusion | flops 4832624640 | bytes 7344128 | tf_op jit(solution)/shard_map/dot_general | solution.py:32
  293.7 1.3 copy.76
  295.0 4.6 all-to-all-start.2
  299.6 0.1 copy.54
  299.7 18.9 %all-to-all-done.2 = f32[384,4,256]{2,0,1:T(8,128)} async-done(((f32[384,4,256]{2,0,1:T(8,128)}), f32[384,4,256]{2,0,1:T(8,128)}, u32[]{:S(2)}, u32[]{:S(2)}) %all-to-all-start.2) | async-done | bytes 1572896 | tf_op jit(solution)/shard_map/all_to_all | solution.py:60
  318.5 5.2 fusion.22
  323.7 8.1 %copy.57 = f32[64,128,256]{2,1,0:T(8,128)} copy(f32[64,128,256]{2,0,1:T(8,128)S(1)} %fusion.22) | data formatting | bytes 16777216 | tf_op jit(solution)/shard_map/db,btf->dtf/dot_general | solution.py:15
  331.8 9.9 %all-to-all-start.3 = ((f32[64,128,256]{2,1,0:T(8,128)}), f32[64,128,256]{2,1,0:T(8,128)}, u32[]{:S(2)}, u32[]{:S(2)}) async-start(f32[64,128,256]{2,1,0:T(8,128)} %copy.57), calls=%async_computation.3 | async-start | bytes 16777216 | tf_op jit(solution)/shard_map/all_to_all | solution.py:16
  341.7 0.3 all-gather.5.cloned.1.call-start
  342.0 0.4 all-gather.5.cloned.1.call-update
  342.4 3.7 copy_multiply_fusion
  346.2 181.2 %all-to-all-done.3 = f32[64,128,256]{2,1,0:T(8,128)} async-done(((f32[64,128,256]{2,1,0:T(8,128)}), f32[64,128,256]{2,1,0:T(8,128)}, u32[]{:S(2)}, u32[]{:S(2)}) %all-to-all-start.3) | async-done | bytes 8388640 | tf_op jit(solution)/shard_map/all_to_all | solution.py:16
  527.4 7.0 %gather_fusion.1 = f32[48,128,256]{2,1,0:T(8,128)} fusion(f32[64,128,256]{2,1,0:T(8,128)} %all-to-all-done.3, s32[1024]{0:T(1024)S(1)} %pad_clamp_fusion), kind=kCustom, calls=%fused_computation.1 | custom fusion | bytes 12583104 | tf_op jit(solution)/shard_map/gather | solution.py:17
  534.4 14.3 %fusion.7 = f32[48,128,256]{1,2,0:T(8,128)} fusion(f32[48,128,256]{2,1,0:T(8,128)} %gather_fusion.1, f32[1,48,128,128]{3,2,1,0:T(8,128)S(1)} %copy-done), kind=kOutput, calls=%fused_computation.7 | convolution fusion | flops 2415919104 | bytes 15728640 | tf_op jit(solution)/shard_map/kij,kjf->kif/dot_general | solution.py:18
  548.7 6.7 %copy.59 = f32[48,128,256]{2,0,1:T(8,128)} copy(f32[48,128,256]{1,2,0:T(8,128)} %fusion.7) | data formatting | bytes 12582912 | tf_op jit(solution)/shard_map/kij,kjf->kif/dot_general | solution.py:18
  555.4 0.0 copy-start.3
  555.4 0.0 copy-start.5
  555.4 4.4 fusion.17
  559.8 0.0 copy-done.3
  559.8 0.0 copy-done.5
  559.8 4.5 bitcast_add_fusion
  564.3 3.1 copy.61
  567.4 2.7 broadcast_multiply_fusion
  570.0 0.0 copy-start.7
  570.0 4.8 all-to-all-start.4
  574.8 0.0 all-gather.5.cloned.1.call-done
  574.8 19.9 %all-to-all-done.4 = f32[4,384,256]{1,2,0:T(8,128)} async-done(((f32[4,384,256]{1,2,0:T(8,128)}), f32[4,384,256]{1,2,0:T(8,128)}, u32[]{:S(2)}, u32[]{:S(2)}) %all-to-all-start.4) | async-done | bytes 1572896 | tf_op jit(solution)/shard_map/all_to_all | solution.py:31
  594.8 0.0 copy-done.7
  594.8 8.3 %convolution_add_fusion = f32[384,1024]{1,0:T(8,128)} fusion(f32[384,1024]{0,1:T(8,128)} %bitcast.21, f32[1024,1024]{1,0:T(8,128)} %all-gather.5.cloned.1.call-done, f32[1024]{0:T(1024)S(1)} %copy-done.7), kind=kOutput, calls=%fused_computation.17 | convolution fusion | flops 4832231424 | bytes 7344128 | tf_op jit(solution)/shard_map/dot_general | solution.py:32
  (3 shorter events, 0.0 us)
Async XLA Ops:
  6.5 220.6 %copy-start = (f32[1,48,128,128]{3,2,1,0:T(8,128)S(1)}, f32[1,48,128,128]{3,2,1,0:T(8,128)}, u32[]{:S(2)}) copy-start(f32[1,48,128,128]{3,2,1,0:T(8,128)} %param.14) | copy-start | bytes 9437188
  6.5 3.8 copy-start.9
  9.2 1.1 copy-start.1
  22.1 13.0 %copy-start.10 = (s32[1,48]{1,0:T(1,128)S(1)}, s32[1,48]{1,0:T(1,128)}, u32[]{:S(2)}) copy-start(s32[1,48]{1,0:T(1,128)} %param.16) | copy-start | bytes 580
  22.1 197.9 %all-to-all-start = ((f32[64,128,256]{2,1,0:T(8,128)}), f32[64,128,256]{2,1,0:T(8,128)}, u32[]{:S(2)}, u32[]{:S(2)}) async-start(f32[64,128,256]{2,1,0:T(8,128)} %copy.48), calls=%async_computation | async-start | bytes 16777216 | tf_op jit(solution)/shard_map/all_to_all | solution.py:16
  34.3 231.9 %all-gather.3.cloned.1.call-start = ((), (), s32[]{:S(2)}) async-start(), calls=%async_computation.5 | async-start | bytes 5242880 | tf_op jit(solution)/shard_map/all_gather | solution.py:34
  241.3 6.7 %copy-start.8 = (s32[1,48]{1,0:T(1,128)S(1)}, s32[1,48]{1,0:T(1,128)}, u32[]{:S(2)}) copy-start(s32[1,48]{1,0:T(1,128)} %param.17) | copy-start | bytes 580
  248.0 4.4 copy-start.2
  248.0 4.4 copy-start.4
  261.7 24.3 %copy-start.6 = (f32[1024]{0:T(1024)S(1)}, f32[1024]{0:T(1024)}, u32[]{:S(2)}) copy-start(f32[1024]{0:T(1024)} %param.19) | copy-start | bytes 12292
  261.7 24.3 %all-to-all-start.1 = ((f32[4,384,256]{1,2,0:T(8,128)}), f32[4,384,256]{1,2,0:T(8,128)}, u32[]{:S(2)}, u32[]{:S(2)}) async-start(f32[4,384,256]{1,2,0:T(8,128)} %broadcast_multiply_fusion.1), calls=%async_computation.1 | async-start | bytes 3145728 | tf_op jit(solution)/shard_map/all_to_all | solution.py:31
  295.0 23.5 %all-to-all-start.2 = ((f32[384,4,256]{2,0,1:T(8,128)}), f32[384,4,256]{2,0,1:T(8,128)}, u32[]{:S(2)}, u32[]{:S(2)}) async-start(f32[384,4,256]{2,0,1:T(8,128)} %bitcast.63), calls=%async_computation.2 | async-start | bytes 3145728 | tf_op jit(solution)/shard_map/all_to_all | solution.py:60
  331.8 195.6 %all-to-all-start.3 = ((f32[64,128,256]{2,1,0:T(8,128)}), f32[64,128,256]{2,1,0:T(8,128)}, u32[]{:S(2)}, u32[]{:S(2)}) async-start(f32[64,128,256]{2,1,0:T(8,128)} %copy.57), calls=%async_computation.3 | async-start | bytes 16777216 | tf_op jit(solution)/shard_map/all_to_all | solution.py:16
  341.7 233.1 %all-gather.5.cloned.1.call-start = ((), (), s32[]{:S(2)}) async-start(), calls=%async_computation.6 | async-start | bytes 5242880 | tf_op jit(solution)/shard_map/all_gather | solution.py:34
  555.4 4.4 copy-start.3
  555.4 4.4 copy-start.5
  570.0 24.8 %copy-start.7 = (f32[1024]{0:T(1024)S(1)}, f32[1024]{0:T(1024)}, u32[]{:S(2)}) copy-start(f32[1024]{0:T(1024)} %param.21) | copy-start | bytes 12292
  570.0 24.8 %all-to-all-start.4 = ((f32[4,384,256]{1,2,0:T(8,128)}), f32[4,384,256]{1,2,0:T(8,128)}, u32[]{:S(2)}, u32[]{:S(2)}) async-start(f32[4,384,256]{1,2,0:T(8,128)} %broadcast_multiply_fusion), calls=%async_computation.4 | async-start | bytes 3145728 | tf_op jit(solution)/shard_map/all_to_all | solution.py:31
Sparse Core Ops, SparseCore 0:
  37.0 51.6 all-gather.2
  344.3 49.6 all-gather.4
where the time goes:
time: 620 us; the launch traced here: 610 us
  waiting for transfers between devices  426 us (69%)
  matrix products  70.2 us (11%)
  local copies, waits for them, and re-layouts  52.3 us (8%)
  starting transfers between devices  36.4 us (6%)
  between operations  14.1 us (2%)
  other arithmetic  11.7 us (2%)
    all_to_all x2, waiting for transfers between devices, aggregate(): lax.all_to_all(outgoing, 'dom', split_axis=0, concat_axis=0, tiled=True)  366 us
    all_to_all x2, waiting for transfers between devices, transform(): lax.all_to_all(aggregated, 'feat', split_axis=0, concat_axis=1, tiled=True)  39.8 us
    dot_general x2, matrix products, aggregate(): jnp.einsum('kij,kjf->kif', remote_adj[0], picked, precision=lax.Precision...  28.5 us
    all_to_all x2, starting transfers between devices, aggregate(): lax.all_to_all(outgoing, 'dom', split_axis=0, concat_axis=0, tiled=True)  22.1 us
    all_to_all x1, waiting for transfers between devices, per_device(): lax.all_to_all(hidden, 'feat', split_axis=1, concat_axis=0, tiled=True)  18.9 us
    dot_general x2, local copies, waits for them, and re-layouts, aggregate(): jnp.einsum('db,btf->dtf', choose, block_rows, precision=lax.Precision.HIG...  16.1 us
    dot_general x2, matrix products, transform(): jnp.dot(vertices, lax.all_gather(weight_rows, 'feat', axis=0, tiled=True)...  15.9 us
    gather x2, local copies, waits for them, and re-layouts, aggregate(): picked = incoming[tile_src[0]]  14.1 us
  transfers between devices with their start and end apart: 7, of which 5 were waited for; matrix products, arithmetic and copies ran while one was open for 14% of the time, Pallas kernels for 0%

commit v1 on v0

v1 whole, which is shorter than its diff:
```python
import functools

import jax
import jax.numpy as jnp
from jax import lax
from jax.experimental import pallas as pl
from jax.experimental.pallas import tpu as pltpu
from jax.sharding import PartitionSpec as P

MESH = pl.DeviceIdType.MESH
F32 = jnp.float32
BF16 = jnp.bfloat16

TILE = 128
BLK = 12
REMOTE = 48
NZ, NX, NC, NY = 8, 4, 2, 4
PLANE = NX * NC
NPARTS = NZ * PLANE
HALF = 128
ROWS = BLK * TILE // NY
READERS = [(1, 0), (3, 0), (1, 1), (3, 1), (2, 0), (2, 1), (0, 1)]


def split(a):
    hi = a.astype(BF16)
    return hi, (a - hi.astype(F32)).astype(BF16)


def dot3(a, b):
    ah, al = split(a)
    bh, bl = split(b)
    out = jnp.dot(ah, bh, preferred_element_type=F32)
    out = out + jnp.dot(ah, bl, preferred_element_type=F32)
    return out + jnp.dot(al, bh, preferred_element_type=F32)


def layer_kernel(
    last_layer,
    tab,
    rbrow,
    feat,
    adj,
    diag,
    scal,
    weight,
    bias,
    out,
    zb00, zb01, zb02, zb10, zb11, zb12,
    zc00, zc01, zc02, zc10, zc11, zc12,
    zfar0, zfar1,
    inc0, inc1,
    sendbuf,
    runs,
    agg0, agg1,
    vert0, vert1,
    wg0, wg1,
    total,
    hid,
    tblv,
    tbls,
    sem_tsend, sem_trecv, sem_tloc,
    sem_zsend, sem_zrecv,
    sem_xsend, sem_xrecv,
    sem_wsend, sem_wrecv,
    sem_ysend, sem_yrecv,
    sem_bsend, sem_brecv,
):
    me = lax.axis_index("dom")
    y = lax.axis_index("feat")
    z = me // PLANE
    xc = lax.rem(me, PLANE)
    x = xc // NC
    c = lax.rem(xc, NC)
    zb = (((zb00, zb01, zb02), (zb10, zb11, zb12)), ((zc00, zc01, zc02), (zc10, zc11, zc12)))
    zfar = (zfar0, zfar1)
    inc = (inc0, inc1)
    agg = (agg0, agg1)
    vert = (vert0, vert1)
    wg = (wg0, wg1)

    def zpeer(step):
        return (lax.rem(z + (step + NZ), NZ) * PLANE + xc, y)

    def reader(dx, dc):
        return lax.rem(x + dx, NX) * NC + lax.rem(c + dc, NC)

    def ypeer(step):
        return lax.rem(y + step, NY)

    barrier = pltpu.get_barrier_semaphore()
    for dz in range(1, NZ):
        pl.semaphore_signal(barrier, inc=1, device_id=zpeer(dz), device_id_type=MESH)
    for dx, dc in READERS:
        pl.semaphore_signal(barrier, inc=1, device_id=(z * PLANE + reader(dx, dc), y), device_id_type=MESH)
    for dy in range(1, NY):
        pl.semaphore_signal(barrier, inc=1, device_id=(me, ypeer(dy)), device_id_type=MESH)
    pl.semaphore_wait(barrier, NZ - 1 + len(READERS) + NY - 1)

    def rdma(src, dst, send, recv, device):
        return pltpu.make_async_remote_copy(
            src_ref=src, dst_ref=dst, send_sem=send, recv_sem=recv, device_id=device, device_id_type=MESH
        )

    table_copies = [
        rdma(rbrow, tblv.at[dz], sem_tsend.at[dz], sem_trecv.at[dz], zpeer(dz)) for dz in range(1, NZ)
    ]
    for copy in table_copies:
        copy.start()
    own_table = pltpu.make_async_copy(rbrow, tbls.at[0], sem_tloc.at[0])
    own_table.start()

    def sub(ref, s):
        return ref.at[pl.ds(s * (BLK // 2), BLK // 2)]

    def own_sub(h, s):
        return feat.at[pl.ds(s * (BLK // 2), BLK // 2), :, pl.ds(h * HALF, HALF)]

    def zbuffer(h, way, d):
        return zfar[h] if d == NZ // 2 else zb[h][way][d - 1]

    def zcopy(h, way, d, s):
        src = own_sub(h, s) if d == 1 else sub(zbuffer(h, way, d - 1), s)
        return rdma(
            src,
            sub(zbuffer(h, way, d), s),
            sem_zsend.at[h, way, d - 1, s],
            sem_zrecv.at[h, way, d - 1, s],
            zpeer(1 if way == 0 else -1),
        )

    def start_own(h):
        for k in range(2):
            for way in range(2):
                zcopy(h, way, 1, k ^ way).start()

    started = []

    def weight_copy(h, dy):
        rows = pl.ds(y * HALF, HALF)
        return rdma(
            weight.at[pl.ds(h * HALF, HALF)],
            wg[h].at[rows],
            sem_wsend.at[h, dy - 1],
            sem_wrecv.at[h, dy - 1],
            (me, ypeer(dy)),
        )

    def serve(h, dz, order, load):
        zs = lax.rem(z + (dz + NZ), NZ)
        slot = zs * PLANE + xc
        entry = (-dz) % NZ
        base = (h * NZ + order) * len(READERS)
        for r, (dx, dc) in enumerate(READERS):
            want = tbls[entry, 0, z * PLANE + reader(dx, dc)]
            sendbuf[base + r] = load(jnp.minimum(want, BLK - 1))
        want = tbls[entry, 0, me]
        inc[h][slot] = load(jnp.minimum(want, BLK - 1))
        for r, (dx, dc) in enumerate(READERS):
            rdma(
                sendbuf.at[base + r],
                inc[h].at[slot],
                sem_xsend.at[h],
                sem_xrecv.at[h],
                (z * PLANE + reader(dx, dc), y),
            ).start()

    def serve_own(h):
        serve(h, 0, 0, lambda b: feat[b, :, h * HALF : (h + 1) * HALF])

    def serve_buffer(h, dz, order, ref):
        serve(h, dz, order, lambda b: ref[b])

    def wait_table(dz):
        table_copies[dz - 1].wait_recv()
        copy = pltpu.make_async_copy(tblv.at[dz], tbls.at[dz], sem_tloc.at[dz])
        copy.start()
        copy.wait()

    def distance(h, d):
        for k in range(2):
            for way in range(2):
                s = k ^ way
                zcopy(h, way, d, s).wait_recv()
                if d < NZ // 2 - 1 or k == 0:
                    zcopy(h, way, d + 1, s).start()
        if h == 0 and d == NZ // 2 - 1:
            start_own(1)
        for way in range(2):
            dz = -d if way == 0 else d
            if h == 0:
                wait_table(-dz % NZ)
            serve_buffer(h, dz, 2 * d - 1 + way, zbuffer(h, way, d))

    def farthest(h):
        d = NZ // 2
        for way in range(2):
            zcopy(h, way, d, way).wait_recv()
        if h == 0:
            wait_table(d)
        serve_buffer(h, d, NZ - 1, zfar[h])

    def ycopy(h, dy):
        n = ypeer(dy)
        return rdma(
            agg[h].at[pl.ds(n * ROWS, ROWS)],
            vert[h].at[:, pl.ds(pl.multiple_of(y * HALF, HALF), HALF)],
            sem_ysend.at[h, dy - 1],
            sem_yrecv.at[h, dy - 1],
            (me, n),
        )

    def aggregate(h):
        many = NPARTS - NZ
        pltpu.make_async_copy(inc[h].at[pl.ds(0, many)], inc[h].at[pl.ds(0, many)], sem_xrecv.at[h]).wait()

        def step(p, acc):
            product = dot3(adj[tab[0, p]], inc[h][tab[1, p]])
            acc = acc * tab[2, p].astype(F32) + product
            runs[p] = acc
            return acc

        lax.fori_loop(0, REMOTE, step, jnp.zeros((TILE, HALF), F32))
        runs[REMOTE] = jnp.zeros((TILE, HALF), F32)
        for dy in (1, 2, 3, 0):
            n = ypeer(dy)

            def finish(j, carry):
                i = n * (BLK // NY) + j
                own = dot3(diag[i], feat[i, :, h * HALF : (h + 1) * HALF])
                value = (own + runs[tab[3, i]]) * scal[i]
                if dy:
                    agg[h][pl.ds(pl.multiple_of(i * TILE, TILE), TILE), :] = value
                else:
                    vert[h][pl.ds(pl.multiple_of(j * TILE, TILE), TILE), pl.ds(pl.multiple_of(y * HALF, HALF), HALF)] = value
                return carry

            lax.fori_loop(0, BLK // NY, finish, 0)
            if dy:
                ycopy(h, dy).start()

    def wait_inputs(h):
        for dy in range(1, NY):
            ycopy(h, dy).wait_recv()
            weight_copy(h, dy).wait_recv()

    def columns(n):
        return pl.ds(pl.multiple_of(n * 256, 256), 256)

    def first_product():
        wait_inputs(0)

        def step(n, carry):
            total[n] = dot3(vert[0][...], wg[0][:, columns(n)]) + bias[:, columns(n)]
            return carry

        lax.fori_loop(0, NY, step, 0)

    def back(n, k):
        return rdma(
            hid.at[n], out.at[pl.ds(y * ROWS, ROWS)], sem_bsend.at[k], sem_brecv.at[k], (me, n)
        )

    def second_product():
        wait_inputs(1)

        def value(n):
            return total[n] + dot3(vert[1][...], wg[1][:, columns(n)])

        if last_layer:

            def step(n, carry):
                out[:, columns(n)] = value(n)
                return carry

            lax.fori_loop(0, NY, step, 0)
            return
        factor = scal[pl.ds(y * (BLK // NY), BLK // NY)].reshape(ROWS, HALF)

        def hidden(n):
            return jnp.maximum(value(n), 0.0) * jnp.concatenate([factor, factor], axis=1)

        def step(k, carry):
            n = ypeer(k + 1)
            hid[n] = hidden(n)
            back(n, k).start()
            return carry

        lax.fori_loop(0, NY - 1, step, 0)
        out[pl.ds(pl.multiple_of(y * ROWS, ROWS), ROWS), :] = hidden(y)
        for k in range(NY - 1):
            back(ypeer(k + 1), k).wait()

    start_own(0)
    for h in range(2):
        for dy in range(1, NY):
            weight_copy(h, dy).start()
    own_table.wait()
    for h in range(2):
        wg[h][pl.ds(pl.multiple_of(y * HALF, HALF), HALF), :] = weight[pl.ds(h * HALF, HALF), :]
    serve_own(0)
    for d in range(1, NZ // 2):
        distance(0, d)
    farthest(0)
    serve_own(1)
    distance(1, 1)
    aggregate(0)
    distance(1, 2)
    first_product()
    distance(1, 3)
    farthest(1)
    aggregate(1)
    second_product()

    for copy in table_copies:
        copy.wait_send()
    for h in range(2):
        for way in range(2):
            for d in range(1, NZ // 2 + 1):
                for s in range(2):
                    if d < NZ // 2 or s == way:
                        zcopy(h, way, d, s).wait_send()
        for dy in range(1, NY):
            weight_copy(h, dy).wait_send()
            ycopy(h, dy).wait_send()
        many = pl.ds(h * NZ * len(READERS), NZ * len(READERS))
        pltpu.make_async_copy(sendbuf.at[many], sendbuf.at[many], sem_xsend.at[h]).wait()


def layer(last_layer, tab, rbrow, feat, adj, diag, scal, weight, bias):
    vmem = pl.BlockSpec(memory_space=pltpu.VMEM)
    smem = pl.BlockSpec(memory_space=pltpu.SMEM)
    dma = pltpu.SemaphoreType.DMA
    chunk = pltpu.VMEM((BLK, TILE, HALF), F32)
    shape = (ROWS, NY * 256) if last_layer else (NY * ROWS, 256)
    return pl.pallas_call(
        functools.partial(layer_kernel, last_layer),
        name="layer_two" if last_layer else "layer_one",
        out_shape=jax.ShapeDtypeStruct(shape, F32),
        in_specs=[smem] + [vmem] * 7,
        out_specs=vmem,
        scratch_shapes=[chunk] * 14
        + [pltpu.VMEM((NPARTS, TILE, HALF), F32)] * 2
        + [
            pltpu.VMEM((2 * NZ * len(READERS), TILE, HALF), F32),
            pltpu.VMEM((REMOTE + 1, TILE, HALF), F32),
        ]
        + [pltpu.VMEM((NY * ROWS, HALF), F32)] * 2
        + [pltpu.VMEM((ROWS, NY * HALF), F32)] * 2
        + [pltpu.VMEM((NY * HALF, 4 * 256), F32)] * 2
        + [
            pltpu.VMEM((NY, ROWS, 256), F32),
            pltpu.VMEM((NY, ROWS, 256), F32),
            pltpu.VMEM((NZ, 8, 128), jnp.int32),
            pltpu.SMEM((NZ, 8, 128), jnp.int32),
            dma((NZ,)),
            dma((NZ,)),
            dma((NZ,)),
            dma((2, 2, 4, 2)),
            dma((2, 2, 4, 2)),
            dma((2,)),
            dma((2,)),
            dma((2, 3)),
            dma((2, 3)),
            dma((2, 3)),
            dma((2, 3)),
            dma((3,)),
            dma((3,)),
        ],
        compiler_params=pltpu.CompilerParams(
            collective_id=int(last_layer), has_side_effects=True, vmem_limit_bytes=63 * 1024 * 1024
        ),
    )(tab, rbrow, feat, adj, diag, scal, weight, bias)


def tile_order(tile_src, tile_row):
    k = jnp.arange(REMOTE, dtype=jnp.int32)
    key = tile_row * REMOTE + k
    rank = jnp.sum((key[None, :] < key[:, None]).astype(jnp.int32), axis=1)
    place = (rank[None, :] == k[:, None]).astype(jnp.int32)
    perm = jnp.sum(place * k[None, :], axis=1)
    source = jnp.sum(place * tile_src[None, :], axis=1)
    row = jnp.sum(place * tile_row[None, :], axis=1)
    same = jnp.concatenate([jnp.zeros((1,), jnp.int32), (row[1:] == row[:-1]).astype(jnp.int32)])
    levels = jnp.arange(BLK, dtype=jnp.int32)
    upto = jnp.sum((tile_row[None, :] <= levels[:, None]).astype(jnp.int32), axis=1)
    here = jnp.sum((tile_row[None, :] == levels[:, None]).astype(jnp.int32), axis=1)
    last = jnp.where(here > 0, upto - 1, REMOTE)
    return jnp.stack([perm, source, same, jnp.pad(last, (0, REMOTE - BLK))])


def per_device(
    features, degree, diag_adj, remote_adj, read_block, tile_src, tile_row, w_first, b_first, w_second, b_second
):
    scaling = lax.rsqrt(degree.astype(F32))
    scaled = features * scaling[:, None]
    scal = jnp.broadcast_to(scaling[:, None], (BLK * TILE, TILE)).reshape(BLK, TILE, TILE)
    tab = tile_order(tile_src[0], tile_row[0])
    rbrow = jnp.zeros((8, 128), jnp.int32).at[0, :NPARTS].set(read_block[0])
    diag = diag_adj.reshape(BLK, TILE, TILE)
    shared = (remote_adj[0], diag, scal)
    hidden = layer(False, tab, rbrow, scaled.reshape(BLK, TILE, 256), *shared, w_first, b_first[None, :])
    return layer(True, tab, rbrow, hidden.reshape(BLK, TILE, 256), *shared, w_second, b_second[None, :])


def solution(mesh):
    return jax.shard_map(
        per_device,
        mesh=mesh,
        in_specs=(
            P("dom", "feat"),
            P("dom"),
            P("dom", None),
            P("dom", None, None, None),
            P("dom", None),
            P("dom", None),
            P("dom", None),
            P("feat", None),
            P(),
            P("feat", None),
            P(),
        ),
        out_specs=P(("dom", "feat"), None),
        check_vma=False,
    )
```

time: 620 us -> 362 us (0.58); the launches traced: 610 us -> 359 us
  waiting for transfers between devices: 426 us -> 0 us
  Pallas kernels: 0 us -> 346 us
  matrix products: 70.2 us -> 0 us
  local copies, waits for them, and re-layouts: 52.3 us -> 5.13 us
  starting transfers between devices: 36.4 us -> 0 us
  between operations: 14.1 us -> 0.03 us
    all_to_all x5 -> x0, waiting for transfers between devices: 425 us -> none  [the longest x2 366 us: aggregate(): lax.all_to_all(outgoing, 'dom', split_axis=0, concat_axis=0, tiled=True)]
    pallas_call x0 -> x2, Pallas kernels: none -> 346 us  [layer(): pl.pallas_call(functools.partial(layer_kernel, last_layer), name='layer_t...]
    dot_general x10 -> x0, matrix products: 70.2 us -> none  [the longest x2 28.5 us: aggregate(): jnp.einsum('kij,kjf->kif', remote_adj[0], picked, precision=lax.Precision...]
    all_to_all x5 -> x0, starting transfers between devices: 35.9 us -> none  [the longest x2 22.1 us: aggregate(): lax.all_to_all(outgoing, 'dom', split_axis=0, concat_axis=0, tiled=True)]
    dot_general x4 -> x0, local copies, waits for them, and re-layouts: 29.5 us -> none  [the longest x2 16.1 us: aggregate(): jnp.einsum('db,btf->dtf', choose, block_rows, precision=lax.Precision.HIG...]
    gather x2 -> x0, local copies, waits for them, and re-layouts: 14.1 us -> none  [aggregate(): picked = incoming[tile_src[0]]]
    mul x5 -> x1, other arithmetic: 11.7 us -> 2.82 us  [per_device(): scaled = features * scaling[:, None]]
  transfers between devices with their start and end apart: 7 -> 0, of which waited for: 5 -> 0; matrix products, arithmetic and copies ran while one was open for 14% -> 0% of each run, Pallas kernels for 0% -> 0%
where the time goes in v1:
time: 362 us; the launch traced here: 359 us
  Pallas kernels  346 us (96%)
  other arithmetic  7.34 us (2%)
  local copies, waits for them, and re-layouts  5.13 us (1%)
    pallas_call x2, Pallas kernels, layer(): pl.pallas_call(functools.partial(layer_kernel, last_layer), name='layer_t...  346 us

profile of v1, /device:TPU:33, one launch (start us, length us, event | category | flops | bytes accessed | tf_op | source)
XLA Modules:
  0.0 358.7 jit_solution(2111066963669370301)
XLA Ops:
  0.0 0.7 iota_add_fusion
  0.7 0.7 add_bitcast_fusion
  1.3 0.2 convert_reduce_fusion
  1.5 0.8 select_reduce_fusion.2
  2.3 0.1 slice_compare_fusion
  2.4 0.1 fusion
  2.5 0.8 convert_reduce_fusion.1
  3.3 0.6 pad_add_fusion.tab
  3.8 1.2 scatter.4.rbrow
  5.1 0.7 fusion.1
  5.8 1.2 broadcast_in_dim.13.scal
  6.9 2.8 broadcast_multiply_fusion
  9.7 184.3 %layer_one.1 = f32[1536,256]{1,0:T(8,128)} custom-call(s32[4,48]{1,0:T(4,128)} %pad_add_fusion.tab, s32[8,128]{1,0:T(8,128)} %scatter.4.rbrow, f32[12,128,256]{2,1,0:T(8,128)} %bitcast.21, f32[48,128,128]{2,1,0:T(8,128)} %bitcast.19, f32[12,128,128]{2,1,0:T(8,128)} %bitcast.23, f32[12,128,128]{2,1,0:T(8,128)} %broadcast_in_dim.13.scal, f32[256,1024]{1,0:T(8,128)} %weight.2, ...), custom_call_target="tpu_custom_call" | custom-call | tf_op jit(solution)/shard_map/layer_one/pallas_call | solution.py:336
  194.0 162.0 %layer_two.1 = f32[384,1024]{1,0:T(8,128)} custom-call(s32[4,48]{1,0:T(4,128)} %pad_add_fusion.tab, s32[8,128]{1,0:T(8,128)} %scatter.4.rbrow, f32[12,128,256]{2,1,0:T(8,128)} %bitcast.22, f32[48,128,128]{2,1,0:T(8,128)} %bitcast.20, f32[12,128,128]{2,1,0:T(8,128)} %bitcast.24, f32[12,128,128]{2,1,0:T(8,128)} %broadcast_in_dim.13.scal, f32[256,1024]{1,0:T(8,128)} %weight.3, ...), custom_call_target="tpu_custom_call" | custom-call | tf_op jit(solution)/shard_map/layer_two/pallas_call | solution.py:336
  356.0 2.7 copy.13
  (2 shorter events, 0.0 us)

commit v2 on v0

v2 whole, which is shorter than its diff:
```python
import functools

import jax
import jax.numpy as jnp
from jax import lax
from jax.experimental import pallas as pl
from jax.experimental.pallas import tpu as pltpu
from jax.sharding import PartitionSpec as P

MESH = pl.DeviceIdType.MESH
F32 = jnp.float32
BF16 = jnp.bfloat16

TILE = 128
BLK = 12
REMOTE = 48
GROUPS = 24
NZ, NX, NC, NY = 8, 4, 2, 4
PLANE = NX * NC
NPARTS = NZ * PLANE
HALF = 128
FEAT = 2 * HALF
SUBS = 2
SUBROWS = TILE // SUBS
NEAR = NZ // 2 - 1
MINE = BLK // NY
ROWS = MINE * TILE
READERS = [(1, 0), (3, 0), (1, 1), (3, 1), (2, 0), (2, 1), (0, 1)]
NREAD = len(READERS)
TABLE_STEPS = [1, 2, 3, NZ - 3, NZ - 2, NZ - 1]
SENDS = SUBS * (NREAD + 2 * (NEAR - 1) * NREAD + 2 * (NREAD + NX))
ARRIVALS = (NZ - 1) * NREAD + PLANE


def split(a):
    hi = a.astype(BF16)
    return hi, (a - hi.astype(F32)).astype(BF16)


def dot3s(ah, al, bh, bl):
    out = jnp.dot(ah, bh, preferred_element_type=F32)
    out = out + jnp.dot(ah, bl, preferred_element_type=F32)
    return out + jnp.dot(al, bh, preferred_element_type=F32)


def dot3(a, b):
    return dot3s(*split(a), *split(b))


def both_layers(*refs):
    refs = list(refs)

    def take(n):
        got = refs[:n]
        del refs[:n]
        return got

    tab, rbrow, degree, raw, adj_hbm, diag, w1, b1, w2, b2, out = take(11)
    zflat = take(2 * 2 * NEAR * SUBS)
    zbuf = [
        [[[zflat[((h * 2 + way) * NEAR + d) * SUBS + s] for s in range(SUBS)] for d in range(NEAR)] for way in range(2)]
        for h in range(2)
    ]
    inc = take(2)
    sendbuf, prod, runs, adjhi, adjlo = take(5)
    agg = take(2)
    vertflat = take(4)
    vert = [vertflat[:2], vertflat[2:]]
    wgflat = take(4)
    wg = [wgflat[:2], wgflat[2:]]
    total, hid = take(2)
    featflat = take(4)
    feats = [featflat[:2], featflat[2:]]
    scal, tblv, tbls = take(3)
    weights = [w1, w2]
    biases = [b1, b2]
    sem_tsend, sem_trecv, sem_tloc, sem_zsend, sem_zrecv, sem_xsend, sem_xrecv = take(7)
    sem_wsend, sem_wrecv, sem_wloc, sem_ysend, sem_yrecv, sem_bsend, sem_brecv, sem_adj, free = take(9)

    me = lax.axis_index("dom")
    y = lax.axis_index("feat")
    z = me // PLANE
    xc = lax.rem(me, PLANE)
    x = xc // NC
    c = lax.rem(xc, NC)

    def plane(step):
        return lax.rem(z + (step + NZ), NZ) * PLANE

    def seat(dx, dc):
        return lax.rem(x + dx, NX) * NC + lax.rem(c + dc, NC)

    def ypeer(step):
        return lax.rem(y + step, NY)

    def rdma(src, dst, send, recv, device):
        return pltpu.make_async_remote_copy(
            src_ref=src, dst_ref=dst, send_sem=send, recv_sem=recv, device_id=device, device_id_type=MESH
        )

    def signal(sem, device):
        pl.semaphore_signal(sem, inc=1, device_id=device, device_id_type=MESH)

    def signal_writers(sem):
        for step in (1, -1):
            signal(sem, (plane(step) + xc, y))
        for dx, dc in READERS:
            signal(sem, (plane(0) + seat(dx, dc), y))
        beyond = lax.rem(z + (2 * c - 1 + NZ), NZ) * PLANE
        for j in range(PLANE):
            signal(sem, (beyond + j, y))

    writers = 2 + NREAD + PLANE

    adj_copy = pltpu.make_async_copy(adj_hbm, prod, sem_adj)
    adj_copy.start()
    own_weights = []
    for l in range(2):
        for h in range(2):
            own_weights.append(
                pltpu.make_async_copy(
                    weights[l].at[pl.ds(h * HALF, HALF)],
                    wg[l][h].at[pl.ds(pl.multiple_of(y * HALF, HALF), HALF)],
                    sem_wloc.at[l, h],
                )
            )
    for copy in own_weights:
        copy.start()
    own_table = pltpu.make_async_copy(rbrow, tbls.at[0], sem_tloc.at[0])
    own_table.start()

    barrier = pltpu.get_barrier_semaphore()
    for dz in TABLE_STEPS[1:-1]:
        signal(barrier, (plane(dz) + xc, y))
    for dy in range(1, NY):
        signal(barrier, (me, ypeer(dy)))
    signal_writers(barrier)

    def scale(i, carry):
        row = lax.rsqrt(degree[pl.ds(i, 1), :].astype(F32))
        scal[i] = jnp.transpose(jnp.broadcast_to(row, (TILE, TILE)))
        factor = scal[i]
        for h in range(2):
            feats[0][h][i] = raw[i, :, h * HALF : (h + 1) * HALF] * factor
        return carry

    lax.fori_loop(0, BLK, scale, 0)
    pl.semaphore_wait(barrier, len(TABLE_STEPS) - 2 + NY - 1 + writers)

    table_copies = {
        dz: rdma(rbrow, tblv.at[dz], sem_tsend.at[dz], sem_trecv.at[dz], (plane(dz) + xc, y)) for dz in TABLE_STEPS
    }

    def wait_table(dz):
        table_copies[dz].wait_recv()
        copy = pltpu.make_async_copy(tblv.at[dz], tbls.at[dz], sem_tloc.at[dz])
        copy.start()
        copy.wait()

    def weight_copy(l, h, dy):
        return rdma(
            weights[l].at[pl.ds(h * HALF, HALF)],
            wg[l][h].at[pl.ds(pl.multiple_of(y * HALF, HALF), HALF)],
            sem_wsend.at[l, h, dy - 1],
            sem_wrecv.at[l, h, dy - 1],
            (me, ypeer(dy)),
        )

    def columns(n):
        return pl.ds(pl.multiple_of(n * FEAT, FEAT), FEAT)

    def run_layer(l):
        feat = feats[l]

        def zcopy(h, way, d, s):
            if d == 1:
                src = feat[h].at[:, pl.ds(s * SUBROWS, SUBROWS)]
            else:
                src = zbuf[h][way][d - 2][s]
            return rdma(
                src,
                zbuf[h][way][d - 1][s],
                sem_zsend.at[h, way, d - 1, s],
                sem_zrecv.at[h, way, d - 1, s],
                (plane(1 if way == 0 else -1) + xc, y),
            )

        def start_own(h):
            for s in range(SUBS):
                for way in range(2):
                    zcopy(h, way, 1, s).start()

        position = [0, 0]

        def serve(h, dz, s, load, beyond=None):
            slot = plane(dz) + xc
            entry = (-dz) % NZ
            rows = pl.ds(s * SUBROWS, SUBROWS)
            targets = []
            if beyond is not None:
                targets = [plane(beyond) + lax.rem(x + dx, NX) * NC + (0 if beyond == 1 else 1) for dx in range(NX)]
            targets = targets + [plane(0) + seat(dx, dc) for dx, dc in READERS]
            base = position[h]
            position[h] += len(targets)
            for r, target in enumerate(targets):
                sendbuf[h * SENDS + base + r] = load(jnp.minimum(tbls[entry, 0, target], BLK - 1))
            inc[h][slot, rows, :] = load(jnp.minimum(tbls[entry, 0, me], BLK - 1))
            for r, target in enumerate(targets):
                rdma(
                    sendbuf.at[h * SENDS + base + r],
                    inc[h].at[slot, rows],
                    sem_xsend.at[h],
                    sem_xrecv.at[h],
                    (target, y),
                ).start()

        def serve_own(h):
            for s in range(SUBS):
                serve(h, 0, s, lambda b: feat[h][b, s * SUBROWS : (s + 1) * SUBROWS, :])

        def distance(h, d):
            for s in range(SUBS):
                for way in range(2):
                    zcopy(h, way, d, s).wait_recv()
                    if d < NEAR:
                        zcopy(h, way, d + 1, s).start()
                if h == 0 and d == NEAR - 1 and s == SUBS - 1:
                    if l == 1:
                        wait_back(1)
                    start_own(1)
                for way in range(2):
                    dz = -d if way == 0 else d
                    if l == 0 and h == 0 and s == 0:
                        wait_table(-dz % NZ)
                    ref = zbuf[h][way][d - 1][s]
                    beyond = None
                    if d == NEAR:
                        beyond = 1 if way == 0 else -1
                    serve(h, dz, s, lambda b: ref[b], beyond)

        def ycopy(h, dy):
            n = ypeer(dy)
            return rdma(
                agg[h].at[pl.ds(pl.multiple_of(n * ROWS, ROWS), ROWS)],
                vert[l][h].at[:, pl.ds(pl.multiple_of(y * HALF, HALF), HALF)],
                sem_ysend.at[h, dy - 1],
                sem_yrecv.at[h, dy - 1],
                (me, n),
            )

        def own_tiles(h):
            def step(i, carry):
                agg[h][pl.ds(pl.multiple_of(i * TILE, TILE), TILE), :] = dot3(
                    diag[i], feat[h][i]
                )
                return carry

            lax.fori_loop(0, BLK, step, 0, unroll=2)

        def aggregate(h):
            many = inc[h].at[pl.ds(0, ARRIVALS)]
            pltpu.make_async_copy(many, many, sem_xrecv.at[h]).wait()

            def group(g, carry):
                block_hi, block_lo = split(inc[h][tab[3, g]])
                pair = dot3s(adjhi[g], adjlo[g], block_hi, block_lo)
                prod[2 * g] = pair[:TILE]
                prod[2 * g + 1] = pair[TILE:]
                return carry

            lax.fori_loop(0, GROUPS, group, 0, unroll=4)

            def run(p, acc):
                acc = acc * tab[1, p].astype(F32) + prod[tab[0, p]]
                runs[p] = acc
                return acc

            lax.fori_loop(0, REMOTE, run, jnp.zeros((TILE, HALF), F32), unroll=4)
            for dy in (1, 2, 3, 0):
                n = ypeer(dy)
                for j in range(MINE):
                    i = n * MINE + j
                    rows = pl.ds(pl.multiple_of(i * TILE, TILE), TILE)
                    value = (agg[h][rows, :] + runs[tab[2, i]]) * scal[i]
                    if dy:
                        agg[h][rows, :] = value
                    else:
                        vert[l][h][j * TILE : (j + 1) * TILE, pl.ds(pl.multiple_of(y * HALF, HALF), HALF)] = value
                if dy:
                    ycopy(h, dy).start()

        def wait_inputs(h):
            own_weights[l * 2 + h].wait()
            for dy in range(1, NY):
                weight_copy(l, h, dy).wait_recv()
            for dy in range(1, NY):
                ycopy(h, dy).wait_recv()

        def first_product():
            wait_inputs(0)

            def step(n, carry):
                total[n] = dot3(vert[l][0][...], wg[l][0][:, columns(n)]) + biases[l][:, columns(n)]
                return carry

            lax.fori_loop(0, NY, step, 0)

        def value(n):
            return total[n] + dot3(vert[l][1][...], wg[l][1][:, columns(n)])

        def last_product():
            wait_inputs(1)

            def step(n, carry):
                out[:, columns(n)] = value(n)
                return carry

            lax.fori_loop(0, NY, step, 0)

        def hidden_product():
            wait_inputs(1)
            factor = scal[pl.ds(y * MINE, MINE)]

            def hidden(n):
                found = jnp.maximum(value(n), 0.0).reshape(MINE, TILE, FEAT)
                return found * jnp.concatenate([factor, factor], axis=2)

            def step(k, carry):
                n = ypeer(k + 1)
                hid[n] = hidden(n)
                back(0, k).start()
                return carry

            lax.fori_loop(0, NY - 1, step, 0)
            for k in range(NY - 1):
                back(1, k).start()
            mine = hidden(y)
            for h in range(2):
                feats[1][h][pl.ds(y * MINE, MINE)] = mine[:, :, h * HALF : (h + 1) * HALF]

        def finish_sends():
            for h in range(2):
                for way in range(2):
                    for d in range(1, NEAR + 1):
                        for s in range(SUBS):
                            zcopy(h, way, d, s).wait_send()
                many = sendbuf.at[pl.ds(h * SENDS, SENDS)]
                pltpu.make_async_copy(many, many, sem_xsend.at[h]).wait()

        def finish_exchange():
            for h in range(2):
                for dy in range(1, NY):
                    ycopy(h, dy).wait_send()
                    weight_copy(l, h, dy).wait_send()

        if l == 1:
            wait_back(0)
            pl.semaphore_wait(free, writers)
        start_own(0)
        if l == 0:
            for copy in table_copies.values():
                copy.start()
            for ll in range(2):
                for h in range(2):
                    for dy in range(1, NY):
                        weight_copy(ll, h, dy).start()
            own_table.wait()
        serve_own(0)
        if l == 0:
            adj_copy.wait()

            def presplit(g, carry):
                for t in range(2):
                    hi, lo = split(prod[2 * g + t])
                    adjhi[g, t * TILE : (t + 1) * TILE, :] = hi
                    adjlo[g, t * TILE : (t + 1) * TILE, :] = lo
                return carry

            lax.fori_loop(0, GROUPS, presplit, 0)
            runs[REMOTE] = jnp.zeros((TILE, HALF), F32)
        own_tiles(0)
        distance(0, 1)
        distance(0, 2)
        distance(0, 3)
        serve_own(1)
        distance(1, 1)
        aggregate(0)
        own_tiles(1)
        distance(1, 2)
        first_product()
        distance(1, 3)
        aggregate(1)
        finish_sends()
        if l == 0:
            signal_writers(free)
            hidden_product()
        else:
            last_product()
        finish_exchange()

    def back(h, k):
        n = ypeer(k + 1)
        cols = pl.ds(h * HALF, HALF)
        return rdma(
            hid.at[n, :, :, cols],
            feats[1][h].at[pl.ds(y * MINE, MINE)],
            sem_bsend.at[h, k],
            sem_brecv.at[h, k],
            (me, n),
        )

    def wait_back(h):
        for k in range(NY - 1):
            back(h, k).wait()

    run_layer(0)
    run_layer(1)
    for copy in table_copies.values():
        copy.wait_send()


def network(tab, rbrow, degree, features, adj, diag, w1, b1, w2, b2):
    vmem = pl.BlockSpec(memory_space=pltpu.VMEM)
    smem = pl.BlockSpec(memory_space=pltpu.SMEM)
    anyw = pl.BlockSpec(memory_space=pl.ANY)
    dma = pltpu.SemaphoreType.DMA
    return pl.pallas_call(
        both_layers,
        name="both_layers",
        out_shape=jax.ShapeDtypeStruct((ROWS, NY * FEAT), F32),
        in_specs=[smem, vmem, vmem, vmem, anyw, vmem, anyw, vmem, anyw, vmem],
        out_specs=vmem,
        scratch_shapes=[pltpu.VMEM((BLK, SUBROWS, HALF), F32)] * (2 * 2 * NEAR * SUBS)
        + [pltpu.VMEM((NPARTS, TILE, HALF), F32)] * 2
        + [
            pltpu.VMEM((2 * SENDS, SUBROWS, HALF), F32),
            pltpu.VMEM((REMOTE, TILE, HALF), F32),
            pltpu.VMEM((REMOTE + 1, TILE, HALF), F32),
            pltpu.VMEM((GROUPS, 2 * TILE, TILE), BF16),
            pltpu.VMEM((GROUPS, 2 * TILE, TILE), BF16),
        ]
        + [pltpu.VMEM((NY * ROWS, HALF), F32)] * 2
        + [pltpu.VMEM((ROWS, NY * HALF), F32)] * 4
        + [pltpu.VMEM((NY * HALF, NY * FEAT), F32)] * 4
        + [
            pltpu.VMEM((NY, ROWS, FEAT), F32),
            pltpu.VMEM((NY, MINE, TILE, FEAT), F32),
        ]
        + [pltpu.VMEM((BLK, TILE, HALF), F32)] * 4
        + [
            pltpu.VMEM((BLK, TILE, TILE), F32),
            pltpu.VMEM((NZ, 8, 128), jnp.int32),
            pltpu.SMEM((NZ, 8, 128), jnp.int32),
            dma((NZ,)),
            dma((NZ,)),
            dma((NZ,)),
            dma((2, 2, NEAR, SUBS)),
            dma((2, 2, NEAR, SUBS)),
            dma((2,)),
            dma((2,)),
            dma((2, 2, 3)),
            dma((2, 2, 3)),
            dma((2, 2)),
            dma((2, 3)),
            dma((2, 3)),
            dma((2, 3)),
            dma((2, 3)),
            dma,
            pltpu.SemaphoreType.REGULAR,
        ],
        compiler_params=pltpu.CompilerParams(
            collective_id=0, has_side_effects=True, vmem_limit_bytes=67_000_000
        ),
    )(tab, rbrow, degree, features, adj, diag, w1, b1, w2, b2)


def prepare_kernel(tile_src, tile_row, read_block, tab, rbrow, place):
    def clear(i, carry):
        place[i] = 0
        tab[2, i] = REMOTE
        return carry

    lax.fori_loop(0, BLK + 1, clear, 0)

    def count(k, carry):
        r = tile_row[0, k] + 1
        place[r] = place[r] + 1
        return carry

    lax.fori_loop(0, REMOTE, count, 0)

    def accumulate(i, carry):
        place[i] = place[i] + place[i - 1]
        return carry

    lax.fori_loop(1, BLK + 1, accumulate, 0)

    def put(k, carry):
        r = tile_row[0, k]
        p = place[r]
        tab[0, p] = k
        tab[1, p] = (tab[2, r] != REMOTE).astype(jnp.int32)
        tab[2, r] = p
        place[r] = p + 1
        return carry

    lax.fori_loop(0, REMOTE, put, 0)

    def source(g, carry):
        tab[3, g] = tile_src[0, 2 * g]
        return carry

    lax.fori_loop(0, GROUPS, source, 0)
    rbrow[0:1, 0:NPARTS] = read_block[...]


def prepare(tile_src, tile_row, read_block):
    vmem = pl.BlockSpec(memory_space=pltpu.VMEM)
    smem = pl.BlockSpec(memory_space=pltpu.SMEM)
    return pl.pallas_call(
        prepare_kernel,
        name="prepare",
        out_shape=(jax.ShapeDtypeStruct((4, 128), jnp.int32), jax.ShapeDtypeStruct((8, 128), jnp.int32)),
        in_specs=[smem, smem, vmem],
        out_specs=(smem, vmem),
        scratch_shapes=[pltpu.SMEM((BLK + 4,), jnp.int32)],
    )(tile_src, tile_row, read_block)


def per_device(
    features, degree, diag_adj, remote_adj, read_block, tile_src, tile_row, w_first, b_first, w_second, b_second
):
    tab, rbrow = prepare(tile_src, tile_row, read_block)
    return network(
        tab,
        rbrow,
        degree.reshape(BLK, TILE),
        features.reshape(BLK, TILE, FEAT),
        remote_adj[0],
        diag_adj.reshape(BLK, TILE, TILE),
        w_first,
        b_first[None, :],
        w_second,
        b_second[None, :],
    )


def solution(mesh):
    return jax.shard_map(
        per_device,
        mesh=mesh,
        in_specs=(
            P("dom", "feat"),
            P("dom"),
            P("dom", None),
            P("dom", None, None, None),
            P("dom", None),
            P("dom", None),
            P("dom", None),
            P("feat", None),
            P(),
            P("feat", None),
            P(),
        ),
        out_specs=P(("dom", "feat"), None),
        check_vma=False,
    )
```

time: 620 us -> 304 us (0.49); the launches traced: 610 us -> 301 us
  waiting for transfers between devices: 426 us -> 0 us
  Pallas kernels: 0 us -> 299 us
  matrix products: 70.2 us -> 0 us
  local copies, waits for them, and re-layouts: 52.3 us -> 2.73 us
  starting transfers between devices: 36.4 us -> 0 us
  between operations: 14.1 us -> 0.02 us
  other arithmetic: 11.7 us -> 0 us
    all_to_all x5 -> x0, waiting for transfers between devices: 425 us -> none  [the longest x2 366 us: aggregate(): lax.all_to_all(outgoing, 'dom', split_axis=0, concat_axis=0, tiled=True)]
    pallas_call x0 -> x2, Pallas kernels: none -> 299 us  [the longest x1 296 us: network(): pl.pallas_call(both_layers, name='both_layers', out_shape=jax.ShapeDtypeS...]
    dot_general x10 -> x0, matrix products: 70.2 us -> none  [the longest x2 28.5 us: aggregate(): jnp.einsum('kij,kjf->kif', remote_adj[0], picked, precision=lax.Precision...]
    all_to_all x5 -> x0, starting transfers between devices: 35.9 us -> none  [the longest x2 22.1 us: aggregate(): lax.all_to_all(outgoing, 'dom', split_axis=0, concat_axis=0, tiled=True)]
    dot_general x4 -> x0, local copies, waits for them, and re-layouts: 29.5 us -> none  [the longest x2 16.1 us: aggregate(): jnp.einsum('db,btf->dtf', choose, block_rows, precision=lax.Precision.HIG...]
    gather x2 -> x0, local copies, waits for them, and re-layouts: 14.1 us -> none  [aggregate(): picked = incoming[tile_src[0]]]
    mul x5 -> x0, other arithmetic: 11.7 us -> none  [the longest x3 6.39 us: aggregate(): scaled = features_slice * scaling[:, None]]
  transfers between devices with their start and end apart: 7 -> 0, of which waited for: 5 -> 0; matrix products, arithmetic and copies ran while one was open for 14% -> 0% of each run, Pallas kernels for 0% -> 0%
where the time goes in v2:
time: 304 us; the launch traced here: 301 us
  Pallas kernels  299 us (98%)
    pallas_call x1, Pallas kernels, network(): pl.pallas_call(both_layers, name='both_layers', out_shape=jax.ShapeDtypeS...  296 us

profile of v2, /device:TPU:33, one launch (start us, length us, event | category | flops | bytes accessed | tf_op | source)
XLA Modules:
  0.0 301.5 jit_solution(2949040531019858485)
XLA Ops:
  0.0 2.7 prepare.1
  2.7 296.0 %both_layers.1 = f32[384,1024]{1,0:T(8,128)} custom-call(s32[4,128]{1,0:T(4,128)} %get-tuple-element.7.refs_0_, s32[8,128]{1,0:T(8,128)} %get-tuple-element.8.refs_1_, s32[12,128]{1,0:T(8,128)} %bitcast.9, f32[12,128,256]{2,1,0:T(8,128)} %bitcast.7, f32[48,128,128]{2,1,0:T(8,128)} %bitcast.6, f32[12,128,128]{2,1,0:T(8,128)} %bitcast.8, f32[256,1024]{1,0:T(8,128)} %refs_6_.1, ...), custom_call_target="tpu_custom_call" | custom-call | tf_op jit(solution)/shard_map/both_layers/pallas_call | solution.py:427
  298.7 2.7 copy.13

commit v3 on v2

--- a/solution.py
+++ b/solution.py
@@ -20,16 +20,14 @@
 NPARTS = NZ * PLANE
 HALF = 128
 FEAT = 2 * HALF
-SUBS = 2
-SUBROWS = TILE // SUBS
-NEAR = NZ // 2 - 1
+NEAR = NZ // 2 - 2
 MINE = BLK // NY
 ROWS = MINE * TILE
 READERS = [(1, 0), (3, 0), (1, 1), (3, 1), (2, 0), (2, 1), (0, 1)]
 NREAD = len(READERS)
-TABLE_STEPS = [1, 2, 3, NZ - 3, NZ - 2, NZ - 1]
-SENDS = SUBS * (NREAD + 2 * (NEAR - 1) * NREAD + 2 * (NREAD + NX))
-ARRIVALS = (NZ - 1) * NREAD + PLANE
+TABLE_STEPS = [1, 2, NZ - 2, NZ - 1]
+SENDS = (1 + 2 * NEAR) * NREAD + 2 * (PLANE + NX)
+ARRIVALS = (1 + 2 * NEAR) * NREAD + 2 * PLANE + PLANE
 
 
 def split(a):
@@ -56,11 +54,8 @@
         return got
 
     tab, rbrow, degree, raw, adj_hbm, diag, w1, b1, w2, b2, out = take(11)
-    zflat = take(2 * 2 * NEAR * SUBS)
-    zbuf = [
-        [[[zflat[((h * 2 + way) * NEAR + d) * SUBS + s] for s in range(SUBS)] for d in range(NEAR)] for way in range(2)]
-        for h in range(2)
-    ]
+    zflat = take(2 * 2 * NEAR)
+    zbuf = [[[zflat[(h * 2 + way) * NEAR + d] for d in range(NEAR)] for way in range(2)] for h in range(2)]
     inc = take(2)
     sendbuf, prod, runs, adjhi, adjlo = take(5)
     agg = take(2)
@@ -102,15 +97,15 @@
         pl.semaphore_signal(sem, inc=1, device_id=device, device_id_type=MESH)
 
     def signal_writers(sem):
-        for step in (1, -1):
-            signal(sem, (plane(step) + xc, y))
         for dx, dc in READERS:
             signal(sem, (plane(0) + seat(dx, dc), y))
-        beyond = lax.rem(z + (2 * c - 1 + NZ), NZ) * PLANE
+        beyond = lax.rem(z + (4 * c - 2 + NZ), NZ) * PLANE
         for j in range(PLANE):
+            signal(sem, (plane(1) + j, y))
+            signal(sem, (plane(-1) + j, y))
             signal(sem, (beyond + j, y))
 
-    writers = 2 + NREAD + PLANE
+    writers = NREAD + 3 * PLANE
 
     adj_copy = pltpu.make_async_copy(adj_hbm, prod, sem_adj)
     adj_copy.start()
@@ -172,71 +167,58 @@
     def run_layer(l):
         feat = feats[l]
 
-        def zcopy(h, way, d, s):
-            if d == 1:
-                src = feat[h].at[:, pl.ds(s * SUBROWS, SUBROWS)]
-            else:
-                src = zbuf[h][way][d - 2][s]
+        def zcopy(h, way, d, part=None):
+            src = feat[h] if d == 1 else zbuf[h][way][d - 2]
+            dst = zbuf[h][way][d - 1]
+            if part is not None:
+                blocks = pl.ds(ypeer(part) * MINE, MINE)
+                src, dst = src.at[blocks], dst.at[blocks]
             return rdma(
                 src,
-                zbuf[h][way][d - 1][s],
-                sem_zsend.at[h, way, d - 1, s],
-                sem_zrecv.at[h, way, d - 1, s],
+                dst,
+                sem_zsend.at[h, way, d - 1],
+                sem_zrecv.at[h, way, d - 1],
                 (plane(1 if way == 0 else -1) + xc, y),
             )
 
-        def start_own(h):
-            for s in range(SUBS):
-                for way in range(2):
-                    zcopy(h, way, 1, s).start()
+        def start_own(h, part=None):
+            for way in range(2):
+                zcopy(h, way, 1, part).start()
 
         position = [0, 0]
 
-        def serve(h, dz, s, load, beyond=None):
+        def serve(h, dz, ref, far=0):
             slot = plane(dz) + xc
             entry = (-dz) % NZ
-            rows = pl.ds(s * SUBROWS, SUBROWS)
             targets = []
-            if beyond is not None:
-                targets = [plane(beyond) + lax.rem(x + dx, NX) * NC + (0 if beyond == 1 else 1) for dx in range(NX)]
-            targets = targets + [plane(0) + seat(dx, dc) for dx, dc in READERS]
-            base = position[h]
+            if far:
+                targets = [plane(2 * far) + lax.rem(x + dx, NX) * NC + (0 if far > 0 else 1) for dx in range(NX)]
+                targets += [plane(far) + seat(dx, dc) for dx, dc in READERS + [(0, 0)]]
+            targets += [plane(0) + seat(dx, dc) for dx, dc in READERS]
+            base = h * SENDS + position[h]
             position[h] += len(targets)
             for r, target in enumerate(targets):
-                sendbuf[h * SENDS + base + r] = load(jnp.minimum(tbls[entry, 0, target], BLK - 1))
-            inc[h][slot, rows, :] = load(jnp.minimum(tbls[entry, 0, me], BLK - 1))
+                sendbuf[base + r] = ref[jnp.minimum(tbls[entry, 0, target], BLK - 1)]
             for r, target in enumerate(targets):
                 rdma(
-                    sendbuf.at[h * SENDS + base + r],
-                    inc[h].at[slot, rows],
+                    sendbuf.at[base + r],
+                    inc[h].at[slot],
                     sem_xsend.at[h],
                     sem_xrecv.at[h],
                     (target, y),
                 ).start()
-
-        def serve_own(h):
-            for s in range(SUBS):
-                serve(h, 0, s, lambda b: feat[h][b, s * SUBROWS : (s + 1) * SUBROWS, :])
+            inc[h][slot] = ref[jnp.minimum(tbls[entry, 0, me], BLK - 1)]
 
         def distance(h, d):
-            for s in range(SUBS):
-                for way in range(2):
-                    zcopy(h, way, d, s).wait_recv()
-                    if d < NEAR:
-                        zcopy(h, way, d + 1, s).start()
-                if h == 0 and d == NEAR - 1 and s == SUBS - 1:
-                    if l == 1:
-                        wait_back(1)
-                    start_own(1)
-                for way in range(2):
-                    dz = -d if way == 0 else d
-                    if l == 0 and h == 0 and s == 0:
-                        wait_table(-dz % NZ)
-                    ref = zbuf[h][way][d - 1][s]
-                    beyond = None
-                    if d == NEAR:
-                        beyond = 1 if way == 0 else -1
-                    serve(h, dz, s, lambda b: ref[b], beyond)
+            for way in range(2):
+                zcopy(h, way, d).wait_recv()
+                if d < NEAR:
+                    zcopy(h, way, d + 1).start()
+            for way in range(2):
+                dz = -d if way == 0 else d
+                if l == 0 and h == 0:
+                    wait_table(-dz % NZ)
+                serve(h, dz, zbuf[h][way][d - 1], (1 if way == 0 else -1) if d == NEAR else 0)
 
         def ycopy(h, dy):
             n = ypeer(dy)
@@ -342,8 +324,7 @@
             for h in range(2):
                 for way in range(2):
                     for d in range(1, NEAR + 1):
-                        for s in range(SUBS):
-                            zcopy(h, way, d, s).wait_send()
+                        zcopy(h, way, d).wait_send()
                 many = sendbuf.at[pl.ds(h * SENDS, SENDS)]
                 pltpu.make_async_copy(many, many, sem_xsend.at[h]).wait()
 
@@ -353,11 +334,9 @@
                     ycopy(h, dy).wait_send()
                     weight_copy(l, h, dy).wait_send()
 
-        if l == 1:
-            wait_back(0)
-            pl.semaphore_wait(free, writers)
-        start_own(0)
         if l == 0:
+            for h in range(2):
+                start_own(h)
             for copy in table_copies.values():
                 copy.start()
             for ll in range(2):
@@ -365,7 +344,17 @@
                     for dy in range(1, NY):
                         weight_copy(ll, h, dy).start()
             own_table.wait()
-        serve_own(0)
+            for h in range(2):
+                serve(h, 0, feat[h])
+        else:
+            pl.semaphore_wait(free, writers)
+            for h in range(2):
+                start_own(h, 0)
+            for h in range(2):
+                for k in range(NY - 1):
+                    back(h, k).wait()
+                    start_own(h, NY - 1 - k)
+                serve(h, 0, feat[h])
         if l == 0:
             adj_copy.wait()
 
@@ -380,15 +369,12 @@
             runs[REMOTE] = jnp.zeros((TILE, HALF), F32)
         own_tiles(0)
         distance(0, 1)
+        distance(1, 1)
+        own_tiles(1)
         distance(0, 2)
-        distance(0, 3)
-        serve_own(1)
-        distance(1, 1)
+        distance(1, 2)
         aggregate(0)
-        own_tiles(1)
-        distance(1, 2)
         first_product()
-        distance(1, 3)
         aggregate(1)
         finish_sends()
         if l == 0:
@@ -408,10 +394,6 @@
             sem_brecv.at[h, k],
             (me, n),
         )
-
-    def wait_back(h):
-        for k in range(NY - 1):
-            back(h, k).wait()
 
     run_layer(0)
     run_layer(1)
@@ -430,10 +412,10 @@
         out_shape=jax.ShapeDtypeStruct((ROWS, NY * FEAT), F32),
         in_specs=[smem, vmem, vmem, vmem, anyw, vmem, anyw, vmem, anyw, vmem],
         out_specs=vmem,
-        scratch_shapes=[pltpu.VMEM((BLK, SUBROWS, HALF), F32)] * (2 * 2 * NEAR * SUBS)
+        scratch_shapes=[pltpu.VMEM((BLK, TILE, HALF), F32)] * (2 * 2 * NEAR)
         + [pltpu.VMEM((NPARTS, TILE, HALF), F32)] * 2
         + [
-            pltpu.VMEM((2 * SENDS, SUBROWS, HALF), F32),
+            pltpu.VMEM((2 * SENDS, TILE, HALF), F32),
             pltpu.VMEM((REMOTE, TILE, HALF), F32),
             pltpu.VMEM((REMOTE + 1, TILE, HALF), F32),
             pltpu.VMEM((GROUPS, 2 * TILE, TILE), BF16),
@@ -454,8 +436,8 @@
             dma((NZ,)),
             dma((NZ,)),
             dma((NZ,)),
-            dma((2, 2, NEAR, SUBS)),
-            dma((2, 2, NEAR, SUBS)),
+            dma((2, 2, NEAR)),
+            dma((2, 2, NEAR)),
             dma((2,)),
             dma((2,)),
             dma((2, 2, 3)),

time: 304 us -> 286 us (0.941)
  Pallas kernels: 299 us -> 280 us
    pallas_call x1, Pallas kernels: 296 us -> 278 us  [network(): pl.pallas_call(both_layers, name='both_layers', out_shape=jax.ShapeDtypeS...]
where the time goes in v3:
time: 286 us; the launch traced here: 283 us
  Pallas kernels  280 us (98%)
    pallas_call x1, Pallas kernels, network(): pl.pallas_call(both_layers, name='both_layers', out_shape=jax.ShapeDtypeS...  278 us

profile of v3, /device:TPU:33, one launch (start us, length us, event | category | flops | bytes accessed | tf_op | source)
XLA Modules:
  0.0 283.0 jit_solution(12273043979369090699)
XLA Ops:
  0.0 2.7 prepare.1
  2.7 277.6 %both_layers.1 = f32[384,1024]{1,0:T(8,128)} custom-call(s32[4,128]{1,0:T(4,128)} %get-tuple-element.7.refs_0_, s32[8,128]{1,0:T(8,128)} %get-tuple-element.8.refs_1_, s32[12,128]{1,0:T(8,128)} %bitcast.9, f32[12,128,256]{2,1,0:T(8,128)} %bitcast.7, f32[48,128,128]{2,1,0:T(8,128)} %bitcast.6, f32[12,128,128]{2,1,0:T(8,128)} %bitcast.8, f32[256,1024]{1,0:T(8,128)} %refs_6_.1, ...), custom_call_target="tpu_custom_call" | custom-call | tf_op jit(solution)/shard_map/both_layers/pallas_call | solution.py:409
  280.3 2.7 copy.13

commit v4 on v3

--- a/solution.py
+++ b/solution.py
@@ -53,7 +53,7 @@
         del refs[:n]
         return got
 
-    tab, rbrow, degree, raw, adj_hbm, diag, w1, b1, w2, b2, out = take(11)
+    tile_src, tile_row, read_block, degree, raw, adj_hbm, diag, w1, b1, w2, b2, out_hbm = take(12)
     zflat = take(2 * 2 * NEAR)
     zbuf = [[[zflat[(h * 2 + way) * NEAR + d] for d in range(NEAR)] for way in range(2)] for h in range(2)]
     inc = take(2)
@@ -66,11 +66,11 @@
     total, hid = take(2)
     featflat = take(4)
     feats = [featflat[:2], featflat[2:]]
-    scal, tblv, tbls = take(3)
+    scal, tblv, tbls, rbrow, tabv, tab, out, verthi, vertlo = take(9)
     weights = [w1, w2]
     biases = [b1, b2]
     sem_tsend, sem_trecv, sem_tloc, sem_zsend, sem_zrecv, sem_xsend, sem_xrecv = take(7)
-    sem_wsend, sem_wrecv, sem_wloc, sem_ysend, sem_yrecv, sem_bsend, sem_brecv, sem_adj, free = take(9)
+    sem_wsend, sem_wrecv, sem_wloc, sem_ysend, sem_yrecv, sem_bsend, sem_brecv, sem_adj, sem_tab, sem_out, free = take(11)
 
     me = lax.axis_index("dom")
     y = lax.axis_index("feat")
@@ -121,9 +121,9 @@
             )
     for copy in own_weights:
         copy.start()
-    own_table = pltpu.make_async_copy(rbrow, tbls.at[0], sem_tloc.at[0])
-    own_table.start()
-
+
+    rbrow[...] = jnp.zeros((8, TILE), jnp.int32)
+    rbrow[0:1, 0:NPARTS] = read_block[...]
     barrier = pltpu.get_barrier_semaphore()
     for dz in TABLE_STEPS[1:-1]:
         signal(barrier, (plane(dz) + xc, y))
@@ -146,9 +146,38 @@
         dz: rdma(rbrow, tblv.at[dz], sem_tsend.at[dz], sem_trecv.at[dz], (plane(dz) + xc, y)) for dz in TABLE_STEPS
     }
 
+    own_table = pltpu.make_async_copy(rbrow, tbls.at[0], sem_tloc.at[0])
+    own_table.start()
+
     def wait_table(dz):
         table_copies[dz].wait_recv()
         copy = pltpu.make_async_copy(tblv.at[dz], tbls.at[dz], sem_tloc.at[dz])
+        copy.start()
+        copy.wait()
+
+    def sort_tiles():
+        lane = lax.broadcasted_iota(jnp.int32, (TILE, TILE), 1)
+        sublane = lax.broadcasted_iota(jnp.int32, (TILE, TILE), 0)
+        tabv[...] = jnp.full((8, TILE), BLK + 1, jnp.int32)
+        tabv[0:1, 0:REMOTE] = tile_row[...]
+        rows = jnp.broadcast_to(tabv[0:1, :], (TILE, TILE))
+        rows_down = jnp.transpose(rows)
+        key, key_down = rows * TILE + lane, rows_down * TILE + sublane
+
+        def total_of(mask, what):
+            return jnp.sum(jnp.where(mask, what, 0), axis=0, keepdims=True)
+
+        rank = total_of(key_down < key, jnp.ones_like(key))
+        rank_down = jnp.transpose(jnp.broadcast_to(rank, (TILE, TILE)))
+        perm = total_of(rank_down == lane, sublane)
+        row = total_of(rank_down == lane, rows_down)
+        before = total_of(rank_down == lane - 1, rows_down)
+        upto = total_of(rows_down <= lane, jnp.ones_like(key))
+        here = total_of(rows_down == lane, jnp.ones_like(key))
+        tabv[0:1, :] = perm
+        tabv[1:2, :] = jnp.where((row == before) & (lane[0:1] > 0), 1, 0)
+        tabv[2:3, :] = jnp.where(here > 0, upto - 1, REMOTE)
+        copy = pltpu.make_async_copy(tabv, tab, sem_tab)
         copy.start()
         copy.wait()
 
@@ -192,8 +221,8 @@
             entry = (-dz) % NZ
             targets = []
             if far:
-                targets = [plane(2 * far) + lax.rem(x + dx, NX) * NC + (0 if far > 0 else 1) for dx in range(NX)]
-                targets += [plane(far) + seat(dx, dc) for dx, dc in READERS + [(0, 0)]]
+                targets = [plane(far) + seat(dx, dc) for dx, dc in READERS + [(0, 0)]]
+                targets += [plane(2 * far) + lax.rem(x + dx, NX) * NC + (0 if far > 0 else 1) for dx in range(NX)]
             targets += [plane(0) + seat(dx, dc) for dx, dc in READERS]
             base = h * SENDS + position[h]
             position[h] += len(targets)
@@ -244,7 +273,7 @@
             pltpu.make_async_copy(many, many, sem_xrecv.at[h]).wait()
 
             def group(g, carry):
-                block_hi, block_lo = split(inc[h][tab[3, g]])
+                block_hi, block_lo = split(inc[h][tile_src[0, 2 * g]])
                 pair = dot3s(adjhi[g], adjlo[g], block_hi, block_lo)
                 prod[2 * g] = pair[:TILE]
                 prod[2 * g + 1] = pair[TILE:]
@@ -278,29 +307,44 @@
             for dy in range(1, NY):
                 ycopy(h, dy).wait_recv()
 
+        def load_inputs(h):
+            wait_inputs(h)
+            hi, lo = split(vert[l][h][...])
+            verthi[...] = hi
+            vertlo[...] = lo
+
+        def product(h, n):
+            return dot3s(verthi[...], vertlo[...], *split(wg[l][h][:, columns(n)]))
+
         def first_product():
-            wait_inputs(0)
+            load_inputs(0)
 
             def step(n, carry):
-                total[n] = dot3(vert[l][0][...], wg[l][0][:, columns(n)]) + biases[l][:, columns(n)]
+                total[n] = product(0, n) + biases[l][:, columns(n)]
                 return carry
 
             lax.fori_loop(0, NY, step, 0)
 
         def value(n):
-            return total[n] + dot3(vert[l][1][...], wg[l][1][:, columns(n)])
+            return total[n] + product(1, n)
+
+        def write(n):
+            return pltpu.make_async_copy(out.at[:, columns(n)], out_hbm.at[:, columns(n)], sem_out.at[n])
 
         def last_product():
-            wait_inputs(1)
+            load_inputs(1)
 
             def step(n, carry):
                 out[:, columns(n)] = value(n)
+                write(n).start()
                 return carry
 
             lax.fori_loop(0, NY, step, 0)
+            for n in range(NY):
+                write(n).wait()
 
         def hidden_product():
-            wait_inputs(1)
+            load_inputs(1)
             factor = scal[pl.ds(y * MINE, MINE)]
 
             def hidden(n):
@@ -368,6 +412,8 @@
             lax.fori_loop(0, GROUPS, presplit, 0)
             runs[REMOTE] = jnp.zeros((TILE, HALF), F32)
         own_tiles(0)
+        if l == 0:
+            sort_tiles()
         distance(0, 1)
         distance(1, 1)
         own_tiles(1)
@@ -401,7 +447,7 @@
         copy.wait_send()
 
 
-def network(tab, rbrow, degree, features, adj, diag, w1, b1, w2, b2):
+def network(*operands):
     vmem = pl.BlockSpec(memory_space=pltpu.VMEM)
     smem = pl.BlockSpec(memory_space=pltpu.SMEM)
     anyw = pl.BlockSpec(memory_space=pl.ANY)
@@ -410,8 +456,8 @@
         both_layers,
         name="both_layers",
         out_shape=jax.ShapeDtypeStruct((ROWS, NY * FEAT), F32),
-        in_specs=[smem, vmem, vmem, vmem, anyw, vmem, anyw, vmem, anyw, vmem],
-        out_specs=vmem,
+        in_specs=[smem, vmem, vmem, vmem, vmem, anyw, vmem, anyw, vmem, anyw, vmem],
+        out_specs=anyw,
         scratch_shapes=[pltpu.VMEM((BLK, TILE, HALF), F32)] * (2 * 2 * NEAR)
         + [pltpu.VMEM((NPARTS, TILE, HALF), F32)] * 2
         + [
@@ -433,6 +479,12 @@
             pltpu.VMEM((BLK, TILE, TILE), F32),
             pltpu.VMEM((NZ, 8, 128), jnp.int32),
             pltpu.SMEM((NZ, 8, 128), jnp.int32),
+            pltpu.VMEM((8, TILE), jnp.int32),
+            pltpu.VMEM((8, TILE), jnp.int32),
+            pltpu.SMEM((8, TILE), jnp.int32),
+            pltpu.VMEM((ROWS, NY * FEAT), F32),
+            pltpu.VMEM((ROWS, NY * HALF), BF16),
+            pltpu.VMEM((ROWS, NY * HALF), BF16),
             dma((NZ,)),
             dma((NZ,)),
             dma((NZ,)),
@@ -448,74 +500,23 @@
             dma((2, 3)),
             dma((2, 3)),
             dma,
+            dma,
+            dma((NY,)),
             pltpu.SemaphoreType.REGULAR,
         ],
         compiler_params=pltpu.CompilerParams(
             collective_id=0, has_side_effects=True, vmem_limit_bytes=67_000_000
         ),
-    )(tab, rbrow, degree, features, adj, diag, w1, b1, w2, b2)
-
-
-def prepare_kernel(tile_src, tile_row, read_block, tab, rbrow, place):
-    def clear(i, carry):
-        place[i] = 0
-        tab[2, i] = REMOTE
-        return carry
-
-    lax.fori_loop(0, BLK + 1, clear, 0)
-
-    def count(k, carry):
-        r = tile_row[0, k] + 1
-        place[r] = place[r] + 1
-        return carry
-
-    lax.fori_loop(0, REMOTE, count, 0)
-
-    def accumulate(i, carry):
-        place[i] = place[i] + place[i - 1]
-        return carry
-
-    lax.fori_loop(1, BLK + 1, accumulate, 0)
-
-    def put(k, carry):
-        r = tile_row[0, k]
-        p = place[r]
-        tab[0, p] = k
-        tab[1, p] = (tab[2, r] != REMOTE).astype(jnp.int32)
-        tab[2, r] = p
-        place[r] = p + 1
-        return carry
-
-    lax.fori_loop(0, REMOTE, put, 0)
-
-    def source(g, carry):
-        tab[3, g] = tile_src[0, 2 * g]
-        return carry
-
-    lax.fori_loop(0, GROUPS, source, 0)
-    rbrow[0:1, 0:NPARTS] = read_block[...]
-
-
-def prepare(tile_src, tile_row, read_block):
-    vmem = pl.BlockSpec(memory_space=pltpu.VMEM)
-    smem = pl.BlockSpec(memory_space=pltpu.SMEM)
-    return pl.pallas_call(
-        prepare_kernel,
-        name="prepare",
-        out_shape=(jax.ShapeDtypeStruct((4, 128), jnp.int32), jax.ShapeDtypeStruct((8, 128), jnp.int32)),
-        in_specs=[smem, smem, vmem],
-        out_specs=(smem, vmem),
-        scratch_shapes=[pltpu.SMEM((BLK + 4,), jnp.int32)],
-    )(tile_src, tile_row, read_block)
+    )(*operands)
 
 
 def per_device(
     features, degree, diag_adj, remote_adj, read_block, tile_src, tile_row, w_first, b_first, w_second, b_second
 ):
-    tab, rbrow = prepare(tile_src, tile_row, read_block)
     return network(
-        tab,
-        rbrow,
+        tile_src,
+        tile_row,
+        read_block,
         degree.reshape(BLK, TILE),
         features.reshape(BLK, TILE, FEAT),
         remote_adj[0],

time: 286 us -> 278 us (0.972)
  Pallas kernels: 280 us -> 275 us
    pallas_call x1, Pallas kernels: 278 us -> 275 us  [network(): pl.pallas_call(both_layers, name='both_layers', out_shape=jax.ShapeDtypeS...]
where the time goes in v4:
time: 278 us; the launch traced here: 277 us
  Pallas kernels  275 us (99%)
    pallas_call x1, Pallas kernels, network(): pl.pallas_call(both_layers, name='both_layers', out_shape=jax.ShapeDtypeS...  275 us

profile of v4, /device:TPU:33, one launch (start us, length us, event | category | flops | bytes accessed | tf_op | source)
XLA Modules:
  0.0 277.3 jit_solution(2922769962346590917)
XLA Ops:
  0.0 274.5 %both_layers.1 = f32[384,1024]{1,0:T(8,128)} custom-call(s32[1,48]{1,0:T(1,128)} %refs_0_.1, s32[1,48]{1,0:T(1,128)} %refs_1_.1, s32[1,64]{1,0:T(1,128)} %refs_2_.1, s32[12,128]{1,0:T(8,128)} %bitcast.9, f32[12,128,256]{2,1,0:T(8,128)} %bitcast.7, f32[48,128,128]{2,1,0:T(8,128)} %bitcast.6, f32[12,128,128]{2,1,0:T(8,128)} %bitcast.8, f32[256,1024]{1,0:T(8,128)} %refs_7_.1, ...), custom_call_target="tpu_custom_call" | custom-call | tf_op jit(solution)/shard_map/both_layers/pallas_call | solution.py:455
  274.5 2.7 copy.13

commit v5 on v4

--- a/solution.py
+++ b/solution.py
@@ -193,26 +193,26 @@
     def columns(n):
         return pl.ds(pl.multiple_of(n * FEAT, FEAT), FEAT)
 
+    def zcopy(l, h, way, d, part=None):
+        src = feats[l][h] if d == 1 else zbuf[h][way][d - 2]
+        dst = zbuf[h][way][d - 1]
+        if part is not None:
+            blocks = pl.ds(ypeer(part) * MINE, MINE)
+            src, dst = src.at[blocks], dst.at[blocks]
+        return rdma(
+            src,
+            dst,
+            sem_zsend.at[h, way, d - 1],
+            sem_zrecv.at[h, way, d - 1],
+            (plane(1 if way == 0 else -1) + xc, y),
+        )
+
+    def start_own(l, h, part=None):
+        for way in range(2):
+            zcopy(l, h, way, 1, part).start()
+
     def run_layer(l):
         feat = feats[l]
-
-        def zcopy(h, way, d, part=None):
-            src = feat[h] if d == 1 else zbuf[h][way][d - 2]
-            dst = zbuf[h][way][d - 1]
-            if part is not None:
-                blocks = pl.ds(ypeer(part) * MINE, MINE)
-                src, dst = src.at[blocks], dst.at[blocks]
-            return rdma(
-                src,
-                dst,
-                sem_zsend.at[h, way, d - 1],
-                sem_zrecv.at[h, way, d - 1],
-                (plane(1 if way == 0 else -1) + xc, y),
-            )
-
-        def start_own(h, part=None):
-            for way in range(2):
-                zcopy(h, way, 1, part).start()
 
         position = [0, 0]
 
@@ -240,9 +240,9 @@
 
         def distance(h, d):
             for way in range(2):
-                zcopy(h, way, d).wait_recv()
+                zcopy(l, h, way, d).wait_recv()
                 if d < NEAR:
-                    zcopy(h, way, d + 1).start()
+                    zcopy(l, h, way, d + 1).start()
             for way in range(2):
                 dz = -d if way == 0 else d
                 if l == 0 and h == 0:
@@ -279,14 +279,14 @@
                 prod[2 * g + 1] = pair[TILE:]
                 return carry
 
-            lax.fori_loop(0, GROUPS, group, 0, unroll=4)
+            lax.fori_loop(0, GROUPS, group, 0, unroll=8)
 
             def run(p, acc):
                 acc = acc * tab[1, p].astype(F32) + prod[tab[0, p]]
                 runs[p] = acc
                 return acc
 
-            lax.fori_loop(0, REMOTE, run, jnp.zeros((TILE, HALF), F32), unroll=4)
+            lax.fori_loop(0, REMOTE, run, jnp.zeros((TILE, HALF), F32), unroll=8)
             for dy in (1, 2, 3, 0):
                 n = ypeer(dy)
                 for j in range(MINE):
@@ -357,18 +357,22 @@
                 back(0, k).start()
                 return carry
 
-            lax.fori_loop(0, NY - 1, step, 0)
+            mine = hidden(y)
+            for h in range(2):
+                feats[1][h][pl.ds(y * MINE, MINE)] = mine[:, :, h * HALF : (h + 1) * HALF]
+            lax.fori_loop(0, 1, step, 0)
+            pl.semaphore_wait(free, writers)
+            for h in range(2):
+                start_own(1, h, 0)
+            lax.fori_loop(1, NY - 1, step, 0)
             for k in range(NY - 1):
                 back(1, k).start()
-            mine = hidden(y)
-            for h in range(2):
-                feats[1][h][pl.ds(y * MINE, MINE)] = mine[:, :, h * HALF : (h + 1) * HALF]
 
         def finish_sends():
             for h in range(2):
                 for way in range(2):
                     for d in range(1, NEAR + 1):
-                        zcopy(h, way, d).wait_send()
+                        zcopy(l, h, way, d).wait_send()
                 many = sendbuf.at[pl.ds(h * SENDS, SENDS)]
                 pltpu.make_async_copy(many, many, sem_xsend.at[h]).wait()
 
@@ -380,7 +384,7 @@
 
         if l == 0:
             for h in range(2):
-                start_own(h)
+                start_own(l, h)
             for copy in table_copies.values():
                 copy.start()
             for ll in range(2):
@@ -391,13 +395,10 @@
             for h in range(2):
                 serve(h, 0, feat[h])
         else:
-            pl.semaphore_wait(free, writers)
-            for h in range(2):
-                start_own(h, 0)
             for h in range(2):
                 for k in range(NY - 1):
                     back(h, k).wait()
-                    start_own(h, NY - 1 - k)
+                    start_own(l, h, NY - 1 - k)
                 serve(h, 0, feat[h])
         if l == 0:
             adj_copy.wait()

time: 278 us -> 276 us (level)
  no operation moved by 1% of the time
where the time goes in v5:
time: 276 us
  Pallas kernels  273 us (99%)
    pallas_call x1, Pallas kernels, network(): pl.pallas_call(both_layers, name='both_layers', out_shape=jax.ShapeDtypeS...  273 us

profile of v5, /device:TPU:33, one launch (start us, length us, event | category | flops | bytes accessed | tf_op | source)
XLA Modules:
  0.0 275.8 jit_solution(6530378347710864984)
XLA Ops:
  0.0 273.0 %both_layers.1 = f32[384,1024]{1,0:T(8,128)} custom-call(s32[1,48]{1,0:T(1,128)} %refs_0_.1, s32[1,48]{1,0:T(1,128)} %refs_1_.1, s32[1,64]{1,0:T(1,128)} %refs_2_.1, s32[12,128]{1,0:T(8,128)} %bitcast.9, f32[12,128,256]{2,1,0:T(8,128)} %bitcast.7, f32[48,128,128]{2,1,0:T(8,128)} %bitcast.6, f32[12,128,128]{2,1,0:T(8,128)} %bitcast.8, f32[256,1024]{1,0:T(8,128)} %refs_7_.1, ...), custom_call_target="tpu_custom_call" | custom-call | tf_op jit(solution)/shard_map/both_layers/pallas_call | solution.py:456
  273.1 2.7 copy.13

commit v6 on v5

--- a/solution.py
+++ b/solution.py
@@ -53,7 +53,7 @@
         del refs[:n]
         return got
 
-    tile_src, tile_row, read_block, degree, raw, adj_hbm, diag, w1, b1, w2, b2, out_hbm = take(12)
+    tile_src, tile_row, read_block, degree, raw, adj_hbm, diag_hbm, w1, b1, w2, b2, out_hbm = take(12)
     zflat = take(2 * 2 * NEAR)
     zbuf = [[[zflat[(h * 2 + way) * NEAR + d] for d in range(NEAR)] for way in range(2)] for h in range(2)]
     inc = take(2)
@@ -66,11 +66,11 @@
     total, hid = take(2)
     featflat = take(4)
     feats = [featflat[:2], featflat[2:]]
-    scal, tblv, tbls, rbrow, tabv, tab, out, verthi, vertlo = take(9)
+    scal, tblv, tbls, rbrow, tabv, tab, out, verthi, vertlo, diag = take(10)
     weights = [w1, w2]
     biases = [b1, b2]
     sem_tsend, sem_trecv, sem_tloc, sem_zsend, sem_zrecv, sem_xsend, sem_xrecv = take(7)
-    sem_wsend, sem_wrecv, sem_wloc, sem_ysend, sem_yrecv, sem_bsend, sem_brecv, sem_adj, sem_tab, sem_out, free = take(11)
+    sem_wsend, sem_wrecv, sem_wloc, sem_ysend, sem_yrecv, sem_bsend, sem_brecv, sem_adj, sem_tab, sem_out, sem_diag, free = take(12)
 
     me = lax.axis_index("dom")
     y = lax.axis_index("feat")
@@ -109,6 +109,8 @@
 
     adj_copy = pltpu.make_async_copy(adj_hbm, prod, sem_adj)
     adj_copy.start()
+    diag_copy = pltpu.make_async_copy(diag_hbm, diag, sem_diag)
+    diag_copy.start()
     own_weights = []
     for l in range(2):
         for h in range(2):
@@ -402,6 +404,7 @@
                 serve(h, 0, feat[h])
         if l == 0:
             adj_copy.wait()
+            diag_copy.wait()
 
             def presplit(g, carry):
                 for t in range(2):
@@ -457,7 +460,7 @@
         both_layers,
         name="both_layers",
         out_shape=jax.ShapeDtypeStruct((ROWS, NY * FEAT), F32),
-        in_specs=[smem, vmem, vmem, vmem, vmem, anyw, vmem, anyw, vmem, anyw, vmem],
+        in_specs=[smem, vmem, vmem, vmem, vmem, anyw, anyw, anyw, vmem, anyw, vmem],
         out_specs=anyw,
         scratch_shapes=[pltpu.VMEM((BLK, TILE, HALF), F32)] * (2 * 2 * NEAR)
         + [pltpu.VMEM((NPARTS, TILE, HALF), F32)] * 2
@@ -486,6 +489,7 @@
             pltpu.VMEM((ROWS, NY * FEAT), F32),
             pltpu.VMEM((ROWS, NY * HALF), BF16),
             pltpu.VMEM((ROWS, NY * HALF), BF16),
+            pltpu.VMEM((BLK, TILE, TILE), F32),
             dma((NZ,)),
             dma((NZ,)),
             dma((NZ,)),
@@ -503,6 +507,7 @@
             dma,
             dma,
             dma((NY,)),
+            dma,
             pltpu.SemaphoreType.REGULAR,
         ],
         compiler_params=pltpu.CompilerParams(

time: 276 us -> 276 us (level)
  no operation moved by 1% of the time
where the time goes in v6:
time: 276 us
  Pallas kernels  273 us (99%)
    pallas_call x1, Pallas kernels, network(): pl.pallas_call(both_layers, name='both_layers', out_shape=jax.ShapeDtypeS...  273 us

profile of v6, /device:TPU:33, one launch (start us, length us, event | category | flops | bytes accessed | tf_op | source)
XLA Modules:
  0.0 275.6 jit_solution(16629113359935741753)
XLA Ops:
  0.0 272.9 %both_layers.1 = f32[384,1024]{1,0:T(8,128)} custom-call(s32[1,48]{1,0:T(1,128)} %refs_0_.1, s32[1,48]{1,0:T(1,128)} %refs_1_.1, s32[1,64]{1,0:T(1,128)} %refs_2_.1, s32[12,128]{1,0:T(8,128)} %bitcast.9, f32[12,128,256]{2,1,0:T(8,128)} %bitcast.7, f32[48,128,128]{2,1,0:T(8,128)} %bitcast.6, f32[12,128,128]{2,1,0:T(8,128)} %bitcast.8, f32[256,1024]{1,0:T(8,128)} %refs_7_.1, ...), custom_call_target="tpu_custom_call" | custom-call | tf_op jit(solution)/shard_map/both_layers/pallas_call | solution.py:459
  272.9 2.7 copy.13
